TPU v7x, 256 devices: a whole 4x4x8 slice. The times are simulated.
256 devices in a mesh: row: 16 (over x, y), col: 16 (over z, core).
Axes of the slice: x: 4, y: 4, z: 8, core: 2. Of those that a mesh axis runs over, the one named last changes fastest.
Arguments:
- features: bfloat16 [65536, 256], P(('col', 'row')), may hold values from -6 to 6
- cotangent: bfloat16 [65536, 256], P(('row', 'col')), may hold values from -1.5 to 1.5
- degrees: int32 [65536], P(('row', 'col')), may hold values from 8 to 40
- weight: bfloat16 [256, 256], replicated, may hold values from -0.375 to 0.375
- tile_rows: int32 [16, 16, 256], P('row', 'col'), may hold values from 0 to 31
- tile_cols: int32 [16, 16, 256], P('row', 'col'), may hold values from 0 to 31
- tile_bits: int32 [16, 16, 256, 16, 128], P('row', 'col'), may hold values from 0 to 255, as said below
- tile_count: int32 [16, 16], P('row', 'col'), may hold values from 16 to 256, as said below
Outputs:
- output: bfloat16 [65536, 256], P(('row', 'col'))
- weight_grad: float32 [256, 256], replicated
- input_grad: bfloat16 [65536, 256], P(('col', 'row'))
Inputs may be any that keep to these rules, and one draw needn't show every extreme that they name: `tile_bits`: each word holds 8 entries of 0 or 1 in its low bits; tiles at the same position may repeat and then add. `tile_count`: some device has all 256 slots live and some device 256 // 16.
All inputs are finite; a program needn't handle non-finite values.
Results may differ from a plain program's by a relative error of at most 0.024.
Values may be sent and summed in bfloat16 or wider, within the bound.
No kernel may reach another device: no remote copies, remote signals or barrier semaphores. Data moves between devices by JAX's collectives and lax.ppermute only.
A program may use at most 64 MiB of HBM per device.

v0:
```python
import math
import jax
import jax.numpy as jnp
from jax import lax
from jax.sharding import PartitionSpec as P


def unpack(packed):
    shifts = jnp.arange(8, dtype=jnp.int32)
    flags = jnp.right_shift(packed[:, :, None, :], shifts[None, None, :, None]) & 1
    return flags.reshape(packed.shape[0], packed.shape[1] * 8, packed.shape[2])


def sweep_tiles(packed, row_ids, col_ids, live_count, source, tile_offset, out_tiles, forward):
    tile_size = packed.shape[-1]
    feature_width = source.shape[-1]
    block_size = math.gcd(packed.shape[0], 32)

    def one_block(position, totals):
        offset = position * block_size
        block_bits = lax.dynamic_slice_in_dim(packed, offset, block_size, 0)
        block_rows = lax.dynamic_slice_in_dim(row_ids, offset, block_size, 0)
        block_cols = lax.dynamic_slice_in_dim(col_ids, offset, block_size, 0)
        if forward:
            target = block_rows - tile_offset
        else:
            target = block_cols - tile_offset
        inside = (target >= 0) & (target < out_tiles)
        live_mask = (offset + jnp.arange(block_size, dtype=jnp.int32) < live_count) & inside
        placed = jnp.clip(target, 0, out_tiles - 1)
        pattern = (unpack(block_bits) * live_mask.astype(jnp.int32)[:, None, None]).astype(
            jnp.bfloat16
        )
        if forward:
            product = jnp.einsum(
                "bji,bjf->bif", pattern, source[block_cols], preferred_element_type=jnp.float32
            )
        else:
            product = jnp.einsum(
                "bji,bif->bjf", pattern, source[block_rows], preferred_element_type=jnp.float32
            )
        return totals.at[placed].add(product)

    initial = jnp.zeros((out_tiles, tile_size, feature_width), jnp.float32)
    blocks_used = packed.shape[0] // block_size
    return lax.fori_loop(0, blocks_used, one_block, initial)


def forward_pass(features, degrees, weight, packed, row_ids, col_ids, live_count):
    tile_size = packed.shape[-1]
    width = features.shape[-1]
    gathered = lax.all_gather(features, "row", axis=0, tiled=True)
    source = gathered.reshape(-1, tile_size, width)
    out_tiles = features.shape[0] * lax.axis_size("col") // tile_size
    partial_value = sweep_tiles(packed, row_ids, col_ids, live_count, source, 0, out_tiles, True)
    summed = lax.psum_scatter(
        partial_value.reshape(-1, width).astype(jnp.bfloat16),
        "col",
        scatter_dimension=0,
        tiled=True,
    ).astype(jnp.float32)
    aggregated = (summed / degrees[:, None].astype(jnp.float32)).astype(jnp.bfloat16)
    output = jnp.dot(aggregated, weight, preferred_element_type=jnp.float32).astype(jnp.bfloat16)
    return (aggregated, output)


def backward_pass(cotangent, degrees, weight, packed, row_ids, col_ids, live_count):
    tile_size = packed.shape[-1]
    width = cotangent.shape[-1]
    scaled = (cotangent.astype(jnp.float32) / degrees[:, None].astype(jnp.float32)).astype(
        jnp.bfloat16
    )
    gathered = lax.all_gather(scaled, "col", axis=0, tiled=True)
    source = gathered.reshape(-1, tile_size, width)
    out_tiles = cotangent.shape[0] * lax.axis_size("row") // tile_size
    partial_value = sweep_tiles(packed, row_ids, col_ids, live_count, source, 0, out_tiles, False)
    summed = lax.psum_scatter(
        partial_value.reshape(-1, width).astype(jnp.bfloat16),
        "row",
        scatter_dimension=0,
        tiled=True,
    )
    return jnp.dot(summed, weight.T, preferred_element_type=jnp.float32).astype(jnp.bfloat16)


def per_device(features, cotangent, degrees, weight, tile_rows, tile_cols, tile_bits, tile_count):
    packed = tile_bits[0, 0]
    row_ids = tile_rows[0, 0]
    col_ids = tile_cols[0, 0]
    live_count = tile_count[0, 0]
    aggregated, output = forward_pass(
        features, degrees, weight, packed, row_ids, col_ids, live_count
    )
    input_grad = backward_pass(cotangent, degrees, weight, packed, row_ids, col_ids, live_count)
    local_term = lax.dot_general(
        aggregated, cotangent, (((0,), (0,)), ((), ())), preferred_element_type=jnp.float32
    )
    weight_grad = lax.psum(local_term, ("row", "col"))
    return (output, weight_grad, input_grad)


def solution(mesh):
    placed = (
        P(("col", "row"), None),
        P(("row", "col"), None),
        P(("row", "col")),
        P(),
        P("row", "col", None),
        P("row", "col", None),
        P("row", "col", None, None, None),
        P("row", "col"),
    )
    return jax.shard_map(
        per_device,
        mesh=mesh,
        in_specs=placed,
        out_specs=(P(("row", "col"), None), P(), P(("col", "row"), None)),
        check_vma=False,
    )
```

profile of v0, /device:TPU:2, one launch (start us, length us, event | category | flops | bytes accessed | tf_op | source)
XLA Modules:
  0.0 690.2 jit_solution(7609712674612229882)
XLA Ops:
  10.4 52.7 %all-gather.3.cloned.1.call-done = bf16[4096,256]{1,0:T(8,128)(2,1)} async-done(((bf16[256,256]{1,0:T(8,128)(2,1)}), bf16[4096,256]{1,0:T(8,128)(2,1)}) %all-gather.3.cloned.1.call-update) | async-done | bytes 2097168 | tf_op jit(solution)/shard_map/all_gather | solution.py:52
  63.1 2.5 broadcast.54.clone
  65.5 136.1 %while.26 = (s32[]{:T(128)}, f32[32,128,256]{2,1,0:T(8,128)}, s32[256]{0:T(256)S(1)}, s32[256,16,128]{2,1,0:T(8,128)}, s32[]{:T(128)}, /*index=5*/s32[256]{0:T(2...) while((s32[]{:T(128)}, f32[32,128,256]{2,1,0:T(8,128)}, ...), condition=%wide.region_2.3_spmd, body=%wide.region_0.2_spmd.sunk | while | flops 271582656 | bytes 23862704 | solution.py:46
  69.7 2.9 fusion.35
  72.6 10.0 %scatter_fusion = f32[32,128,256]{2,1,0:T(8,128)} fusion(f32[32,128,256]{2,1,0:T(8,128)} %get-tuple-element.398, s32[32]{0:T(128)S(1)} %get-tuple-element.375, f32[32,128,256]{2,1,0:T(8,128)} %fusion.35), kind=kCustom, calls=%fused_computation.2.clone.1 | custom fusion | flops 1048576 | bytes 12583040 | tf_op jit(solution)/shard_map/while/body/eval_jaxpr/scatter-add | solution.py:42
  86.8 2.9 fusion.35
  89.7 10.0 %scatter_fusion = f32[32,128,256]{2,1,0:T(8,128)} fusion(f32[32,128,256]{2,1,0:T(8,128)} %get-tuple-element.398, s32[32]{0:T(128)S(1)} %get-tuple-element.375, f32[32,128,256]{2,1,0:T(8,128)} %fusion.35), kind=kCustom, calls=%fused_computation.2.clone.1 | custom fusion | flops 1048576 | bytes 12583040 | tf_op jit(solution)/shard_map/while/body/eval_jaxpr/scatter-add | solution.py:42
  100.5 2.3 gather_fusion
  103.9 2.9 fusion.35
  106.8 9.8 %scatter_fusion = f32[32,128,256]{2,1,0:T(8,128)} fusion(f32[32,128,256]{2,1,0:T(8,128)} %get-tuple-element.398, s32[32]{0:T(128)S(1)} %get-tuple-element.375, f32[32,128,256]{2,1,0:T(8,128)} %fusion.35), kind=kCustom, calls=%fused_computation.2.clone.1 | custom fusion | flops 1048576 | bytes 12583040 | tf_op jit(solution)/shard_map/while/body/eval_jaxpr/scatter-add | solution.py:42
  120.7 2.9 fusion.35
  123.6 9.9 %scatter_fusion = f32[32,128,256]{2,1,0:T(8,128)} fusion(f32[32,128,256]{2,1,0:T(8,128)} %get-tuple-element.398, s32[32]{0:T(128)S(1)} %get-tuple-element.375, f32[32,128,256]{2,1,0:T(8,128)} %fusion.35), kind=kCustom, calls=%fused_computation.2.clone.1 | custom fusion | flops 1048576 | bytes 12583040 | tf_op jit(solution)/shard_map/while/body/eval_jaxpr/scatter-add | solution.py:42
  137.7 2.9 fusion.35
  140.6 9.9 %scatter_fusion = f32[32,128,256]{2,1,0:T(8,128)} fusion(f32[32,128,256]{2,1,0:T(8,128)} %get-tuple-element.398, s32[32]{0:T(128)S(1)} %get-tuple-element.375, f32[32,128,256]{2,1,0:T(8,128)} %fusion.35), kind=kCustom, calls=%fused_computation.2.clone.1 | custom fusion | flops 1048576 | bytes 12583040 | tf_op jit(solution)/shard_map/while/body/eval_jaxpr/scatter-add | solution.py:42
  151.3 2.3 gather_fusion
  154.6 2.9 fusion.35
  157.5 10.0 %scatter_fusion = f32[32,128,256]{2,1,0:T(8,128)} fusion(f32[32,128,256]{2,1,0:T(8,128)} %get-tuple-element.398, s32[32]{0:T(128)S(1)} %get-tuple-element.375, f32[32,128,256]{2,1,0:T(8,128)} %fusion.35), kind=kCustom, calls=%fused_computation.2.clone.1 | custom fusion | flops 1048576 | bytes 12583040 | tf_op jit(solution)/shard_map/while/body/eval_jaxpr/scatter-add | solution.py:42
  171.7 2.9 fusion.35
  174.6 10.0 %scatter_fusion = f32[32,128,256]{2,1,0:T(8,128)} fusion(f32[32,128,256]{2,1,0:T(8,128)} %get-tuple-element.398, s32[32]{0:T(128)S(1)} %get-tuple-element.375, f32[32,128,256]{2,1,0:T(8,128)} %fusion.35), kind=kCustom, calls=%fused_computation.2.clone.1 | custom fusion | flops 1048576 | bytes 12583040 | tf_op jit(solution)/shard_map/while/body/eval_jaxpr/scatter-add | solution.py:42
  188.8 2.9 fusion.35
  191.7 9.9 %scatter_fusion = f32[32,128,256]{2,1,0:T(8,128)} fusion(f32[32,128,256]{2,1,0:T(8,128)} %get-tuple-element.398, s32[32]{0:T(128)S(1)} %get-tuple-element.375, f32[32,128,256]{2,1,0:T(8,128)} %fusion.35), kind=kCustom, calls=%fused_computation.2.clone.1 | custom fusion | flops 1048576 | bytes 12583040 | tf_op jit(solution)/shard_map/while/body/eval_jaxpr/scatter-add | solution.py:42
  201.6 3.8 convert_element_type.63
  205.5 2.5 broadcast.54.clone.1
  208.0 134.8 %while.27 = (s32[]{:T(128)}, f32[32,128,256]{2,1,0:T(8,128)}, s32[256]{0:T(256)S(1)}, s32[256,16,128]{2,1,0:T(8,128)}, s32[]{:T(128)}, /*index=5*/s32[256]{0:T(2...) while((s32[]{:T(128)}, f32[32,128,256]{2,1,0:T(8,128)}, ...), condition=%wide.region_7.8_spmd, body=%wide.region_5.7_spmd.sunk | while | flops 271582656 | bytes 23862704 | solution.py:46
  208.8 2.3 gather_fusion.1
  212.2 2.7 fusion.38
  214.9 10.2 %scatter_fusion.1 = f32[32,128,256]{2,1,0:T(8,128)} fusion(f32[32,128,256]{2,1,0:T(8,128)} %get-tuple-element.431, s32[32]{0:T(128)S(1)} %get-tuple-element.384, f32[32,128,256]{2,1,0:T(8,128)} %fusion.38), kind=kCustom, calls=%fused_computation.3.clone.1 | custom fusion | flops 1048576 | bytes 12583040 | tf_op jit(solution)/shard_map/while/body/eval_jaxpr/scatter-add | solution.py:42
  229.3 2.7 fusion.38
  232.0 9.8 %scatter_fusion.1 = f32[32,128,256]{2,1,0:T(8,128)} fusion(f32[32,128,256]{2,1,0:T(8,128)} %get-tuple-element.431, s32[32]{0:T(128)S(1)} %get-tuple-element.384, f32[32,128,256]{2,1,0:T(8,128)} %fusion.38), kind=kCustom, calls=%fused_computation.3.clone.1 | custom fusion | flops 1048576 | bytes 12583040 | tf_op jit(solution)/shard_map/while/body/eval_jaxpr/scatter-add | solution.py:42
  242.6 2.3 gather_fusion.1
  246.0 2.7 fusion.38
  248.7 10.0 %scatter_fusion.1 = f32[32,128,256]{2,1,0:T(8,128)} fusion(f32[32,128,256]{2,1,0:T(8,128)} %get-tuple-element.431, s32[32]{0:T(128)S(1)} %get-tuple-element.384, f32[32,128,256]{2,1,0:T(8,128)} %fusion.38), kind=kCustom, calls=%fused_computation.3.clone.1 | custom fusion | flops 1048576 | bytes 12583040 | tf_op jit(solution)/shard_map/while/body/eval_jaxpr/scatter-add | solution.py:42
  259.5 2.3 gather_fusion.1
  262.8 2.7 fusion.38
  265.5 9.9 %scatter_fusion.1 = f32[32,128,256]{2,1,0:T(8,128)} fusion(f32[32,128,256]{2,1,0:T(8,128)} %get-tuple-element.431, s32[32]{0:T(128)S(1)} %get-tuple-element.384, f32[32,128,256]{2,1,0:T(8,128)} %fusion.38), kind=kCustom, calls=%fused_computation.3.clone.1 | custom fusion | flops 1048576 | bytes 12583040 | tf_op jit(solution)/shard_map/while/body/eval_jaxpr/scatter-add | solution.py:42
  276.2 2.3 gather_fusion.1
  279.6 2.7 fusion.38
  282.3 9.9 %scatter_fusion.1 = f32[32,128,256]{2,1,0:T(8,128)} fusion(f32[32,128,256]{2,1,0:T(8,128)} %get-tuple-element.431, s32[32]{0:T(128)S(1)} %get-tuple-element.384, f32[32,128,256]{2,1,0:T(8,128)} %fusion.38), kind=kCustom, calls=%fused_computation.3.clone.1 | custom fusion | flops 1048576 | bytes 12583040 | tf_op jit(solution)/shard_map/while/body/eval_jaxpr/scatter-add | solution.py:42
  296.3 2.7 fusion.38
  299.0 10.0 %scatter_fusion.1 = f32[32,128,256]{2,1,0:T(8,128)} fusion(f32[32,128,256]{2,1,0:T(8,128)} %get-tuple-element.431, s32[32]{0:T(128)S(1)} %get-tuple-element.384, f32[32,128,256]{2,1,0:T(8,128)} %fusion.38), kind=kCustom, calls=%fused_computation.3.clone.1 | custom fusion | flops 1048576 | bytes 12583040 | tf_op jit(solution)/shard_map/while/body/eval_jaxpr/scatter-add | solution.py:42
  309.8 2.3 gather_fusion.1
  313.2 2.7 fusion.38
  315.9 10.1 %scatter_fusion.1 = f32[32,128,256]{2,1,0:T(8,128)} fusion(f32[32,128,256]{2,1,0:T(8,128)} %get-tuple-element.431, s32[32]{0:T(128)S(1)} %get-tuple-element.384, f32[32,128,256]{2,1,0:T(8,128)} %fusion.38), kind=kCustom, calls=%fused_computation.3.clone.1 | custom fusion | flops 1048576 | bytes 12583040 | tf_op jit(solution)/shard_map/while/body/eval_jaxpr/scatter-add | solution.py:42
  330.1 2.7 fusion.38
  332.8 10.0 %scatter_fusion.1 = f32[32,128,256]{2,1,0:T(8,128)} fusion(f32[32,128,256]{2,1,0:T(8,128)} %get-tuple-element.431, s32[32]{0:T(128)S(1)} %get-tuple-element.384, f32[32,128,256]{2,1,0:T(8,128)} %fusion.38), kind=kCustom, calls=%fused_computation.3.clone.1 | custom fusion | flops 1048576 | bytes 12583040 | tf_op jit(solution)/shard_map/while/body/eval_jaxpr/scatter-add | solution.py:42
  342.9 3.8 convert_element_type.71
  351.4 73.8 %reduce-scatter.5.cloned.1.call-done = bf16[256,256]{1,0:T(8,128)(2,1)} async-done(((bf16[4096,256]{1,0:T(8,128)(2,1)}), bf16[256,256]{1,0:T(8,128)(2,1)}) %reduce-scatter.5.cloned.1.call-update) | async-done | bytes 131088 | tf_op jit(solution)/shard_map/reduce_scatter | solution.py:77
  426.9 255.1 %all-reduce.2.cloned.1.call-done = f32[256,256]{1,0:T(8,128)} async-done(((f32[256,256]{1,0:T(8,128)}), f32[256,256]{1,0:T(8,128)}) %all-reduce.2.cloned.1.call-update) | async-done | bytes 262160 | tf_op jit(solution)/shard_map/psum | solution.py:98
  (131 shorter events, 61.7 us)
Async XLA Ops:
  7.2 342.4 %copy-start = (bf16[256,256]{1,0:T(8,128)(2,1)S(1)}, bf16[256,256]{1,0:T(8,128)(2,1)}, u32[]{:S(2)}) copy-start(bf16[256,256]{1,0:T(8,128)(2,1)} %param.15) | copy-start | bytes 393220
  7.2 55.9 %all-gather.3.cloned.1.call-start = ((), (), s32[]{:S(2)}) async-start(), calls=%async_computation.2 | async-start | bytes 2228224 | tf_op jit(solution)/shard_map/all_gather | solution.py:52
  7.9 197.6 %all-gather.5.cloned.1.call-start = ((), (), s32[]{:S(2)}) async-start(), calls=%async_computation.5 | async-start | bytes 2228224 | tf_op jit(solution)/shard_map/all_gather | solution.py:73
  10.3 336.5 %reduce-scatter.3.cloned.1.call-start = ((), (), s32[]{:S(2)}) async-start(), calls=%async_computation.3 | async-start | bytes 2228224 | tf_op jit(solution)/shard_map/reduce_scatter | solution.py:56
  63.1 2.5 copy-start.2
  63.1 2.5 copy-start.3
  205.5 219.7 %reduce-scatter.5.cloned.1.call-start = ((), (), s32[]{:S(2)}) async-start(), calls=%async_computation.6 | async-start | bytes 2228224 | tf_op jit(solution)/shard_map/reduce_scatter | solution.py:77
  346.7 0.9 copy-start.1
  346.7 335.2 %all-reduce.2.cloned.1.call-start = ((), (), s32[]{:S(2)}) async-start(), calls=%async_computation.4 | async-start | bytes 524288 | tf_op jit(solution)/shard_map/psum | solution.py:98
Sparse Core Ops, SparseCore 0:
  10.4 52.5 all-gather.2
  65.5 39.5 all-gather.4
  205.6 59.0 reduce-scatter.2
  346.9 78.2 reduce-scatter.4
  431.9 250.0 all-reduce.1
where the time goes:
time: 692 us; the launch traced here: 690 us
  waiting for transfers between devices  382 us (55%)
  other arithmetic  182 us (26%)
  local copies, waits for them, and re-layouts  60.8 us (9%)
  matrix products  50.3 us (7%)
  between operations  13.8 us (2%)
    psum x1, waiting for transfers between devices, per_device(): weight_grad = lax.psum(local_term, ('row', 'col'))  255 us
    scatter-add x16, other arithmetic, one_block(): return totals.at[placed].add(product)  159 us
    reduce_scatter x1, waiting for transfers between devices, backward_pass(): lax.psum_scatter(partial_value.reshape(-1, width).astype(jnp.bfloat16), '...  73.8 us
    all_gather x1, waiting for transfers between devices, forward_pass(): gathered = lax.all_gather(features, 'row', axis=0, tiled=True)  52.7 us
    dot_general x8, matrix products, one_block(): jnp.einsum('bji,bjf->bif', pattern, source[block_cols], preferred_element...  23.2 us
    dot_general x8, matrix products, one_block(): jnp.einsum('bji,bif->bjf', pattern, source[block_rows], preferred_element...  21.6 us
    gather x8, local copies, waits for them, and re-layouts, one_block(): source[block_rows]  18.2 us
    gather x8, local copies, waits for them, and re-layouts, one_block(): source[block_cols]  18.2 us
  transfers between devices with their start and end apart: 5, of which 3 were waited for; matrix products, arithmetic and copies ran while one was open for 42% of the time, Pallas kernels for 0%

commit v1 on v0

--- a/solution.py
+++ b/solution.py
@@ -3,6 +3,11 @@
 import jax.numpy as jnp
 from jax import lax
 from jax.sharding import PartitionSpec as P
+
+
+def one_after_other(x, inner_axis, outer_axis):
+    inner = lax.psum(x, inner_axis)
+    return lax.psum(inner, outer_axis)
 
 
 def unpack(packed):
@@ -95,7 +100,7 @@
     local_term = lax.dot_general(
         aggregated, cotangent, (((0,), (0,)), ((), ())), preferred_element_type=jnp.float32
     )
-    weight_grad = lax.psum(local_term, ("row", "col"))
+    weight_grad = one_after_other(local_term, "row", "col")
     return (output, weight_grad, input_grad)
 
 

time: 692 us -> 645 us (0.932)
  waiting for transfers between devices: 382 us -> 336 us
    psum x1 -> x2, waiting for transfers between devices: 255 us -> 109 us  [the longest x1 109 us: one_after_other(): return lax.psum(inner, outer_axis)]
    reduce_scatter x1, waiting for transfers between devices: 0.02 us -> 57.5 us  [forward_pass(): lax.psum_scatter(partial_value.reshape(-1, width).astype(jnp.bfloat16), '...]
    all_gather x1, waiting for transfers between devices: 0.02 us -> 38.7 us  [backward_pass(): gathered = lax.all_gather(scaled, 'col', axis=0, tiled=True)]
  transfers between devices with their start and end apart: 5 -> 6, of which waited for: 3 -> 5; matrix products, arithmetic and copies ran while one was open for 42% -> 23% of each run, Pallas kernels for 0% -> 0%
where the time goes in v1:
time: 645 us; the launch traced here: 643 us
  waiting for transfers between devices  336 us (52%)
  other arithmetic  181 us (28%)
  local copies, waits for them, and re-layouts  61.6 us (10%)
  matrix products  49.6 us (8%)
  between operations  14.1 us (2%)
    scatter-add x16, other arithmetic, one_block(): return totals.at[placed].add(product)  159 us
    psum x1, waiting for transfers between devices, one_after_other(): return lax.psum(inner, outer_axis)  109 us
    reduce_scatter x1, waiting for transfers between devices, backward_pass(): lax.psum_scatter(partial_value.reshape(-1, width).astype(jnp.bfloat16), '...  75.7 us
    reduce_scatter x1, waiting for transfers between devices, forward_pass(): lax.psum_scatter(partial_value.reshape(-1, width).astype(jnp.bfloat16), '...  57.5 us
    all_gather x1, waiting for transfers between devices, forward_pass(): gathered = lax.all_gather(features, 'row', axis=0, tiled=True)  55.1 us
    all_gather x1, waiting for transfers between devices, backward_pass(): gathered = lax.all_gather(scaled, 'col', axis=0, tiled=True)  38.7 us
    dot_general x8, matrix products, one_block(): jnp.einsum('bji,bjf->bif', pattern, source[block_cols], preferred_element...  23.3 us
    dot_general x8, matrix products, one_block(): jnp.einsum('bji,bif->bjf', pattern, source[block_rows], preferred_element...  21.7 us
  transfers between devices with their start and end apart: 6, of which 5 were waited for; matrix products, arithmetic and copies ran while one was open for 23% of the time, Pallas kernels for 0%

profile of v1, /device:TPU:2, one launch (start us, length us, event | category | flops | bytes accessed | tf_op | source)
XLA Modules:
  0.0 642.8 jit_solution(17190796132954499026)
XLA Ops:
  8.0 55.1 %all-gather.3.cloned.1.call-done = bf16[4096,256]{1,0:T(8,128)(2,1)} async-done(((bf16[256,256]{1,0:T(8,128)(2,1)}), bf16[4096,256]{1,0:T(8,128)(2,1)}) %all-gather.3.cloned.1.call-update) | async-done | bytes 2097168 | tf_op jit(solution)/shard_map/all_gather | solution.py:57
  63.1 2.5 broadcast.54.clone
  65.5 136.1 %while.26 = (s32[]{:T(128)}, f32[32,128,256]{2,1,0:T(8,128)}, s32[256]{0:T(256)S(1)}, s32[256,16,128]{2,1,0:T(8,128)}, s32[]{:T(128)}, /*index=5*/s32[256]{0:T(2...) while((s32[]{:T(128)}, f32[32,128,256]{2,1,0:T(8,128)}, ...), condition=%wide.region_2.3_spmd, body=%wide.region_0.2_spmd.sunk | while | flops 271582656 | bytes 23862704 | solution.py:51
  69.7 2.9 fusion.35
  72.6 10.0 %scatter_fusion = f32[32,128,256]{2,1,0:T(8,128)} fusion(f32[32,128,256]{2,1,0:T(8,128)} %get-tuple-element.398, s32[32]{0:T(128)S(1)} %get-tuple-element.375, f32[32,128,256]{2,1,0:T(8,128)} %fusion.35), kind=kCustom, calls=%fused_computation.2.clone.1 | custom fusion | flops 1048576 | bytes 12583040 | tf_op jit(solution)/shard_map/while/body/eval_jaxpr/scatter-add | solution.py:47
  86.8 2.9 fusion.35
  89.7 10.0 %scatter_fusion = f32[32,128,256]{2,1,0:T(8,128)} fusion(f32[32,128,256]{2,1,0:T(8,128)} %get-tuple-element.398, s32[32]{0:T(128)S(1)} %get-tuple-element.375, f32[32,128,256]{2,1,0:T(8,128)} %fusion.35), kind=kCustom, calls=%fused_computation.2.clone.1 | custom fusion | flops 1048576 | bytes 12583040 | tf_op jit(solution)/shard_map/while/body/eval_jaxpr/scatter-add | solution.py:47
  100.4 2.3 gather_fusion
  103.8 2.9 fusion.35
  106.7 9.8 %scatter_fusion = f32[32,128,256]{2,1,0:T(8,128)} fusion(f32[32,128,256]{2,1,0:T(8,128)} %get-tuple-element.398, s32[32]{0:T(128)S(1)} %get-tuple-element.375, f32[32,128,256]{2,1,0:T(8,128)} %fusion.35), kind=kCustom, calls=%fused_computation.2.clone.1 | custom fusion | flops 1048576 | bytes 12583040 | tf_op jit(solution)/shard_map/while/body/eval_jaxpr/scatter-add | solution.py:47
  120.6 2.9 fusion.35
  123.5 9.9 %scatter_fusion = f32[32,128,256]{2,1,0:T(8,128)} fusion(f32[32,128,256]{2,1,0:T(8,128)} %get-tuple-element.398, s32[32]{0:T(128)S(1)} %get-tuple-element.375, f32[32,128,256]{2,1,0:T(8,128)} %fusion.35), kind=kCustom, calls=%fused_computation.2.clone.1 | custom fusion | flops 1048576 | bytes 12583040 | tf_op jit(solution)/shard_map/while/body/eval_jaxpr/scatter-add | solution.py:47
  137.7 2.9 fusion.35
  140.6 9.8 %scatter_fusion = f32[32,128,256]{2,1,0:T(8,128)} fusion(f32[32,128,256]{2,1,0:T(8,128)} %get-tuple-element.398, s32[32]{0:T(128)S(1)} %get-tuple-element.375, f32[32,128,256]{2,1,0:T(8,128)} %fusion.35), kind=kCustom, calls=%fused_computation.2.clone.1 | custom fusion | flops 1048576 | bytes 12583040 | tf_op jit(solution)/shard_map/while/body/eval_jaxpr/scatter-add | solution.py:47
  154.6 2.9 fusion.35
  157.5 10.0 %scatter_fusion = f32[32,128,256]{2,1,0:T(8,128)} fusion(f32[32,128,256]{2,1,0:T(8,128)} %get-tuple-element.398, s32[32]{0:T(128)S(1)} %get-tuple-element.375, f32[32,128,256]{2,1,0:T(8,128)} %fusion.35), kind=kCustom, calls=%fused_computation.2.clone.1 | custom fusion | flops 1048576 | bytes 12583040 | tf_op jit(solution)/shard_map/while/body/eval_jaxpr/scatter-add | solution.py:47
  168.3 2.3 gather_fusion
  171.6 2.9 fusion.35
  174.5 10.1 %scatter_fusion = f32[32,128,256]{2,1,0:T(8,128)} fusion(f32[32,128,256]{2,1,0:T(8,128)} %get-tuple-element.398, s32[32]{0:T(128)S(1)} %get-tuple-element.375, f32[32,128,256]{2,1,0:T(8,128)} %fusion.35), kind=kCustom, calls=%fused_computation.2.clone.1 | custom fusion | flops 1048576 | bytes 12583040 | tf_op jit(solution)/shard_map/while/body/eval_jaxpr/scatter-add | solution.py:47
  188.8 2.9 fusion.35
  191.7 9.9 %scatter_fusion = f32[32,128,256]{2,1,0:T(8,128)} fusion(f32[32,128,256]{2,1,0:T(8,128)} %get-tuple-element.398, s32[32]{0:T(128)S(1)} %get-tuple-element.375, f32[32,128,256]{2,1,0:T(8,128)} %fusion.35), kind=kCustom, calls=%fused_computation.2.clone.1 | custom fusion | flops 1048576 | bytes 12583040 | tf_op jit(solution)/shard_map/while/body/eval_jaxpr/scatter-add | solution.py:47
  201.6 3.8 convert_element_type.63
  207.2 57.5 %reduce-scatter.3.cloned.1.call-done = bf16[256,256]{1,0:T(8,128)(2,1)} async-done(((bf16[4096,256]{1,0:T(8,128)(2,1)}), bf16[256,256]{1,0:T(8,128)(2,1)}) %reduce-scatter.3.cloned.1.call-update) | async-done | bytes 131088 | tf_op jit(solution)/shard_map/reduce_scatter | solution.py:61
  266.6 38.7 %all-gather.5.cloned.1.call-done = bf16[4096,256]{1,0:T(8,128)(2,1)} async-done(((bf16[256,256]{1,0:T(8,128)(2,1)}), bf16[4096,256]{1,0:T(8,128)(2,1)}) %all-gather.5.cloned.1.call-update) | async-done | bytes 2097168 | tf_op jit(solution)/shard_map/all_gather | solution.py:78
  305.3 2.5 broadcast.54.clone.1
  307.8 134.8 %while.27 = (s32[]{:T(128)}, f32[32,128,256]{2,1,0:T(8,128)}, s32[256]{0:T(256)S(1)}, s32[256,16,128]{2,1,0:T(8,128)}, s32[]{:T(128)}, /*index=5*/s32[256]{0:T(2...) while((s32[]{:T(128)}, f32[32,128,256]{2,1,0:T(8,128)}, ...), condition=%wide.region_8.9_spmd, body=%wide.region_6.0_spmd.sunk | while | flops 271582656 | bytes 23862704 | solution.py:51
  308.6 2.3 gather_fusion.1
  311.9 2.7 fusion.38
  314.6 10.1 %scatter_fusion.1 = f32[32,128,256]{2,1,0:T(8,128)} fusion(f32[32,128,256]{2,1,0:T(8,128)} %get-tuple-element.431, s32[32]{0:T(128)S(1)} %get-tuple-element.384, f32[32,128,256]{2,1,0:T(8,128)} %fusion.38), kind=kCustom, calls=%fused_computation.3.clone.1 | custom fusion | flops 1048576 | bytes 12583040 | tf_op jit(solution)/shard_map/while/body/eval_jaxpr/scatter-add | solution.py:47
  325.6 2.3 gather_fusion.1
  328.9 2.7 fusion.38
  331.7 9.8 %scatter_fusion.1 = f32[32,128,256]{2,1,0:T(8,128)} fusion(f32[32,128,256]{2,1,0:T(8,128)} %get-tuple-element.431, s32[32]{0:T(128)S(1)} %get-tuple-element.384, f32[32,128,256]{2,1,0:T(8,128)} %fusion.38), kind=kCustom, calls=%fused_computation.3.clone.1 | custom fusion | flops 1048576 | bytes 12583040 | tf_op jit(solution)/shard_map/while/body/eval_jaxpr/scatter-add | solution.py:47
  345.6 2.7 fusion.38
  348.3 9.9 %scatter_fusion.1 = f32[32,128,256]{2,1,0:T(8,128)} fusion(f32[32,128,256]{2,1,0:T(8,128)} %get-tuple-element.431, s32[32]{0:T(128)S(1)} %get-tuple-element.384, f32[32,128,256]{2,1,0:T(8,128)} %fusion.38), kind=kCustom, calls=%fused_computation.3.clone.1 | custom fusion | flops 1048576 | bytes 12583040 | tf_op jit(solution)/shard_map/while/body/eval_jaxpr/scatter-add | solution.py:47
  362.4 2.7 fusion.38
  365.1 9.9 %scatter_fusion.1 = f32[32,128,256]{2,1,0:T(8,128)} fusion(f32[32,128,256]{2,1,0:T(8,128)} %get-tuple-element.431, s32[32]{0:T(128)S(1)} %get-tuple-element.384, f32[32,128,256]{2,1,0:T(8,128)} %fusion.38), kind=kCustom, calls=%fused_computation.3.clone.1 | custom fusion | flops 1048576 | bytes 12583040 | tf_op jit(solution)/shard_map/while/body/eval_jaxpr/scatter-add | solution.py:47
  379.2 2.7 fusion.38
  381.9 9.9 %scatter_fusion.1 = f32[32,128,256]{2,1,0:T(8,128)} fusion(f32[32,128,256]{2,1,0:T(8,128)} %get-tuple-element.431, s32[32]{0:T(128)S(1)} %get-tuple-element.384, f32[32,128,256]{2,1,0:T(8,128)} %fusion.38), kind=kCustom, calls=%fused_computation.3.clone.1 | custom fusion | flops 1048576 | bytes 12583040 | tf_op jit(solution)/shard_map/while/body/eval_jaxpr/scatter-add | solution.py:47
  392.6 2.3 gather_fusion.1
  395.9 2.7 fusion.38
  398.7 10.1 %scatter_fusion.1 = f32[32,128,256]{2,1,0:T(8,128)} fusion(f32[32,128,256]{2,1,0:T(8,128)} %get-tuple-element.431, s32[32]{0:T(128)S(1)} %get-tuple-element.384, f32[32,128,256]{2,1,0:T(8,128)} %fusion.38), kind=kCustom, calls=%fused_computation.3.clone.1 | custom fusion | flops 1048576 | bytes 12583040 | tf_op jit(solution)/shard_map/while/body/eval_jaxpr/scatter-add | solution.py:47
  412.9 2.7 fusion.38
  415.6 10.1 %scatter_fusion.1 = f32[32,128,256]{2,1,0:T(8,128)} fusion(f32[32,128,256]{2,1,0:T(8,128)} %get-tuple-element.431, s32[32]{0:T(128)S(1)} %get-tuple-element.384, f32[32,128,256]{2,1,0:T(8,128)} %fusion.38), kind=kCustom, calls=%fused_computation.3.clone.1 | custom fusion | flops 1048576 | bytes 12583040 | tf_op jit(solution)/shard_map/while/body/eval_jaxpr/scatter-add | solution.py:47
  429.8 2.7 fusion.38
  432.5 10.0 %scatter_fusion.1 = f32[32,128,256]{2,1,0:T(8,128)} fusion(f32[32,128,256]{2,1,0:T(8,128)} %get-tuple-element.431, s32[32]{0:T(128)S(1)} %get-tuple-element.384, f32[32,128,256]{2,1,0:T(8,128)} %fusion.38), kind=kCustom, calls=%fused_computation.3.clone.1 | custom fusion | flops 1048576 | bytes 12583040 | tf_op jit(solution)/shard_map/while/body/eval_jaxpr/scatter-add | solution.py:47
  442.5 3.8 convert_element_type.71
  448.2 75.7 %reduce-scatter.5.cloned.1.call-done = bf16[256,256]{1,0:T(8,128)(2,1)} async-done(((bf16[4096,256]{1,0:T(8,128)(2,1)}), bf16[256,256]{1,0:T(8,128)(2,1)}) %reduce-scatter.5.cloned.1.call-update) | async-done | bytes 131088 | tf_op jit(solution)/shard_map/reduce_scatter | solution.py:82
  525.7 108.6 %all-reduce.5.cloned.1.call-done = f32[256,256]{1,0:T(8,128)} async-done(((f32[256,256]{1,0:T(8,128)}), f32[256,256]{1,0:T(8,128)}) %all-reduce.5.cloned.1.call-update) | async-done | bytes 262160 | tf_op jit(solution)/shard_map/psum | solution.py:10
  (138 shorter events, 64.6 us)
Async XLA Ops:
  7.2 439.3 %copy-start = (bf16[256,256]{1,0:T(8,128)(2,1)S(1)}, bf16[256,256]{1,0:T(8,128)(2,1)}, u32[]{:S(2)}) copy-start(bf16[256,256]{1,0:T(8,128)(2,1)} %param.15) | copy-start | bytes 393220
  7.2 55.9 %all-gather.3.cloned.1.call-start = ((), (), s32[]{:S(2)}) async-start(), calls=%async_computation.2 | async-start | bytes 2228224 | tf_op jit(solution)/shard_map/all_gather | solution.py:57
  7.9 256.7 %reduce-scatter.3.cloned.1.call-start = ((), (), s32[]{:S(2)}) async-start(), calls=%async_computation.3 | async-start | bytes 2228224 | tf_op jit(solution)/shard_map/reduce_scatter | solution.py:61
  63.1 2.5 copy-start.2
  63.1 2.5 copy-start.3
  205.4 0.7 copy-start.4
  205.4 0.9 copy-start.1
  205.5 99.9 %all-gather.5.cloned.1.call-start = ((), (), s32[]{:S(2)}) async-start(), calls=%async_computation.6 | async-start | bytes 2228224 | tf_op jit(solution)/shard_map/all_gather | solution.py:78
  207.1 241.0 %all-reduce.3.cloned.1.call-start = ((), (), s32[]{:S(2)}) async-start(), calls=%async_computation.4 | async-start | bytes 524288 | tf_op jit(solution)/shard_map/psum | solution.py:9
  266.6 257.3 %reduce-scatter.5.cloned.1.call-start = ((), (), s32[]{:S(2)}) async-start(), calls=%async_computation.7 | async-start | bytes 2228224 | tf_op jit(solution)/shard_map/reduce_scatter | solution.py:82
  446.4 0.9 copy-start.5
  446.4 187.9 %all-reduce.5.cloned.1.call-start = ((), (), s32[]{:S(2)}) async-start(), calls=%async_computation.5 | async-start | bytes 524288 | tf_op jit(solution)/shard_map/psum | solution.py:10
Sparse Core Ops, SparseCore 0:
  10.4 52.5 all-gather.2
  205.6 59.0 reduce-scatter.2
  267.1 38.2 all-gather.4
  308.9 92.3 all-reduce.2
  446.5 77.3 reduce-scatter.4
  526.1 108.1 all-reduce.4
